TPU v7x, 32 devices: a whole 2x2x4 slice. The times are simulated.
32 devices in a mesh: gx: 2 (over core), gy: 4 (over y, x), gz: 4 (over z).
Axes of the slice: x: 2, y: 2, z: 4, core: 2. Of those that a mesh axis runs over, the one named last changes fastest.
Arguments:
- right_side: float32 [64, 512, 256], P('gx', 'gy', 'gz'), may hold values from -21 to 21, as said below
- conductivity: float32 [64, 512, 256], P('gx', 'gy', 'gz'), may hold values from 0.25 to 1
- absorption: float32 [64, 512, 256], P('gx', 'gy', 'gz'), may hold values from 0.5 to 2
Outputs:
- solution_field: float32 [64, 512, 256], P('gx', 'gy', 'gz')
- residual: float32 [64, 512, 256], P('gx', 'gy', 'gz')
Inputs may be any that keep to these rules, and one draw needn't show every extreme that they name: right_side lies within -21 and 21.
All inputs are finite; a program needn't handle non-finite values.
Results may differ from a plain program's by a relative error of at most 0.004.
Values sent between devices are 32-bit elements.
A program may use at most 128 MiB of HBM per device.

v0:
```python
import jax
import jax.numpy as jnp
from jax import lax
from jax.sharding import PartitionSpec as P

ITERS = 10


def padded_2(cells, sides, width, closed):
    for axis, dim in sides:
        count = lax.axis_size(axis)
        ends = count if closed else count - 1
        head = lax.slice_in_dim(cells, 0, width, axis=dim)
        tail = lax.slice_in_dim(cells, cells.shape[dim] - width, cells.shape[dim], axis=dim)
        cells = jnp.concatenate(
            [
                lax.ppermute(tail, axis, [(i, (i + 1) % count) for i in range(ends)]),
                cells,
                lax.ppermute(head, axis, [((i + 1) % count, i) for i in range(ends)]),
            ],
            axis=dim,
        )
    return cells


def coefficients(conductivity, absorption):
    padded = padded_2(conductivity, (("gx", 0), ("gy", 1), ("gz", 2)), 1, False)
    face_x = 0.5 * (padded[:-1, 1:-1, 1:-1] + padded[1:, 1:-1, 1:-1])
    face_y = 0.5 * (padded[1:-1, :-1, 1:-1] + padded[1:-1, 1:, 1:-1])
    face_z = 0.5 * (padded[1:-1, 1:-1, :-1] + padded[1:-1, 1:-1, 1:])
    total = (
        absorption
        + face_x[1:]
        + face_x[:-1]
        + face_y[:, 1:]
        + face_y[:, :-1]
        + face_z[:, :, 1:]
        + face_z[:, :, :-1]
    )
    return (face_x, face_y, face_z, total)


def operate(field, coeffs):
    face_x, face_y, face_z, total = coeffs
    padded = padded_2(field, (("gx", 0), ("gy", 1), ("gz", 2)), 1, False)
    beside = face_x[1:] * padded[2:, 1:-1, 1:-1] + face_x[:-1] * padded[:-2, 1:-1, 1:-1]
    beside = (
        beside + face_y[:, 1:] * padded[1:-1, 2:, 1:-1] + face_y[:, :-1] * padded[1:-1, :-2, 1:-1]
    )
    beside = (
        beside
        + face_z[:, :, 1:] * padded[1:-1, 1:-1, 2:]
        + face_z[:, :, :-1] * padded[1:-1, 1:-1, :-2]
    )
    return total * field - beside


def paired_dots(residual, precond, image):
    return lax.psum((jnp.sum(residual * precond), jnp.sum(precond * image)), ("gx", "gy", "gz"))


def local(right_side, conductivity, absorption):
    coeffs = coefficients(conductivity, absorption)
    total = coeffs[3]
    solution_field = jnp.zeros_like(right_side)
    residual = right_side
    precond = residual / total
    image = operate(precond, coeffs)
    rho_now, product = paired_dots(residual, precond, image)
    step_size = rho_now / product
    direction = precond
    along = image
    for iteration in range(ITERS):
        solution_field = solution_field + step_size * direction
        residual = residual - step_size * along
        if iteration + 1 < ITERS:
            precond = residual / total
            image = operate(precond, coeffs)
            rho_next, product = paired_dots(residual, precond, image)
            mixing = rho_next / rho_now
            step_size = rho_next / (product - mixing * rho_next / step_size)
            direction = precond + mixing * direction
            along = image + mixing * along
            rho_now = rho_next
    return (solution_field, residual)


def solution(mesh):
    return jax.shard_map(
        local,
        mesh=mesh,
        in_specs=(P("gx", "gy", "gz"), P("gx", "gy", "gz"), P("gx", "gy", "gz")),
        out_specs=(P("gx", "gy", "gz"), P("gx", "gy", "gz")),
        check_vma=False,
    )
```

profile of v0, /device:TPU:0, one launch (start us, length us, event | category | flops | bytes accessed | tf_op | source)
XLA Modules:
  0.0 904.5 jit_solution(3954952273287613782)
XLA Ops:
  13.5 4.9 collective-permute-start.2
  24.4 4.6 collective-permute-start.4
  42.0 4.7 collective-permute-start.9
  68.6 7.7 multiply_reduce_fusion.18
  76.3 40.7 %all-reduce.9 = (f32[]{:T(128)}, f32[]{:T(128)}) all-reduce(f32[]{:T(128)} %get-tuple-element.27, f32[]{:T(128)} %get-tuple-element.26), channel_id=1, replica_groups=mesh['gx'=2,'gy'=4,'gz'=4] {'gx','gy','gz'}, use_global_device_ids=true, to_apply=%region_1.0 | all-reduce | flops 2 | bytes 16 | tf_op jit(solution)/shard_map/psum | solution.py:59
  152.2 7.8 multiply_reduce_fusion.16
  160.0 40.1 %all-reduce.8 = (f32[]{:T(128)}, f32[]{:T(128)}) all-reduce(f32[]{:T(128)} %get-tuple-element.25, f32[]{:T(128)} %get-tuple-element.24), channel_id=1, replica_groups=mesh['gx'=2,'gy'=4,'gz'=4] {'gx','gy','gz'}, use_global_device_ids=true, to_apply=%region_5.0 | all-reduce | flops 2 | bytes 16 | tf_op jit(solution)/shard_map/psum | solution.py:59
  239.1 7.8 multiply_reduce_fusion.14
  246.9 40.1 %all-reduce.7 = (f32[]{:T(128)}, f32[]{:T(128)}) all-reduce(f32[]{:T(128)} %get-tuple-element.23, f32[]{:T(128)} %get-tuple-element.22), channel_id=1, replica_groups=mesh['gx'=2,'gy'=4,'gz'=4] {'gx','gy','gz'}, use_global_device_ids=true, to_apply=%region_9.0 | all-reduce | flops 2 | bytes 16 | tf_op jit(solution)/shard_map/psum | solution.py:59
  326.0 7.7 multiply_reduce_fusion.12
  333.7 40.1 %all-reduce.6 = (f32[]{:T(128)}, f32[]{:T(128)}) all-reduce(f32[]{:T(128)} %get-tuple-element.21, f32[]{:T(128)} %get-tuple-element.20), channel_id=1, replica_groups=mesh['gx'=2,'gy'=4,'gz'=4] {'gx','gy','gz'}, use_global_device_ids=true, to_apply=%region_13.0 | all-reduce | flops 2 | bytes 16 | tf_op jit(solution)/shard_map/psum | solution.py:59
  411.9 7.7 multiply_reduce_fusion.10
  419.5 40.1 %all-reduce.5 = (f32[]{:T(128)}, f32[]{:T(128)}) all-reduce(f32[]{:T(128)} %get-tuple-element.19, f32[]{:T(128)} %get-tuple-element.18), channel_id=1, replica_groups=mesh['gx'=2,'gy'=4,'gz'=4] {'gx','gy','gz'}, use_global_device_ids=true, to_apply=%region_17.0 | all-reduce | flops 2 | bytes 16 | tf_op jit(solution)/shard_map/psum | solution.py:59
  499.1 7.7 multiply_reduce_fusion.8
  506.7 40.1 %all-reduce.4 = (f32[]{:T(128)}, f32[]{:T(128)}) all-reduce(f32[]{:T(128)} %get-tuple-element.17, f32[]{:T(128)} %get-tuple-element.16), channel_id=1, replica_groups=mesh['gx'=2,'gy'=4,'gz'=4] {'gx','gy','gz'}, use_global_device_ids=true, to_apply=%region_21.0 | all-reduce | flops 2 | bytes 16 | tf_op jit(solution)/shard_map/psum | solution.py:59
  585.4 7.7 multiply_reduce_fusion.6
  593.1 40.2 %all-reduce.3 = (f32[]{:T(128)}, f32[]{:T(128)}) all-reduce(f32[]{:T(128)} %get-tuple-element.15, f32[]{:T(128)} %get-tuple-element.14), channel_id=1, replica_groups=mesh['gx'=2,'gy'=4,'gz'=4] {'gx','gy','gz'}, use_global_device_ids=true, to_apply=%region_25.0 | all-reduce | flops 2 | bytes 16 | tf_op jit(solution)/shard_map/psum | solution.py:59
  672.5 7.7 multiply_reduce_fusion.4
  680.1 40.1 %all-reduce.2 = (f32[]{:T(128)}, f32[]{:T(128)}) all-reduce(f32[]{:T(128)} %get-tuple-element.13, f32[]{:T(128)} %get-tuple-element.12), channel_id=1, replica_groups=mesh['gx'=2,'gy'=4,'gz'=4] {'gx','gy','gz'}, use_global_device_ids=true, to_apply=%region_29.0 | all-reduce | flops 2 | bytes 16 | tf_op jit(solution)/shard_map/psum | solution.py:59
  758.3 7.6 multiply_reduce_fusion.2
  765.9 40.1 %all-reduce.1 = (f32[]{:T(128)}, f32[]{:T(128)}) all-reduce(f32[]{:T(128)} %get-tuple-element.11, f32[]{:T(128)} %get-tuple-element.10), channel_id=1, replica_groups=mesh['gx'=2,'gy'=4,'gz'=4] {'gx','gy','gz'}, use_global_device_ids=true, to_apply=%region_33.0 | all-reduce | flops 2 | bytes 16 | tf_op jit(solution)/shard_map/psum | solution.py:59
  844.3 8.0 multiply_reduce_fusion
  852.4 40.1 %all-reduce = (f32[]{:T(128)}, f32[]{:T(128)}) all-reduce(f32[]{:T(128)} %get-tuple-element.9, f32[]{:T(128)} %get-tuple-element.8), channel_id=1, replica_groups=mesh['gx'=2,'gy'=4,'gz'=4] {'gx','gy','gz'}, use_global_device_ids=true, to_apply=%region_37.0 | all-reduce | flops 2 | bytes 16 | tf_op jit(solution)/shard_map/psum | solution.py:59
  896.2 6.6 multiply_add_fusion
  (355 shorter events, 366.6 us)
Async XLA Ops:
  12.2 8.1 collective-permute-start.3
  13.5 6.3 collective-permute-start.2
  23.1 6.6 collective-permute-start.5
  24.4 6.3 collective-permute-start.4
  42.0 7.7 collective-permute-start.9
  48.4 6.9 collective-permute-start.8
  58.4 5.9 collective-permute-start.11
  62.7 5.9 collective-permute-start.10
  129.1 7.5 collective-permute-start.15
  146.3 5.9 collective-permute-start.16
  215.9 7.6 collective-permute-start.21
  233.1 5.9 collective-permute-start.22
  302.9 7.6 collective-permute-start.27
  320.1 5.9 collective-permute-start.28
  388.7 7.6 collective-permute-start.33
  405.9 5.9 collective-permute-start.34
  475.9 7.6 collective-permute-start.39
  493.1 5.9 collective-permute-start.40
  562.2 7.6 collective-permute-start.45
  649.3 7.5 collective-permute-start.51
  666.5 5.9 collective-permute-start.52
  735.2 7.5 collective-permute-start.57
  821.2 7.5 collective-permute-start.63
  838.4 5.9 collective-permute-start.64
  (81 other events, 466.7 us)
where the time goes:
time: 917 us; the launch traced here: 905 us
  blocking collectives  402 us (44%)
  other arithmetic  140 us (15%)
  starting transfers between devices  138 us (15%)
  waiting for transfers between devices  95.5 us (10%)
  local copies, waits for them, and re-layouts  91.1 us (10%)
  between operations  38 us (4%)
    psum x10, blocking collectives, paired_dots(): lax.psum((jnp.sum(residual * precond), jnp.sum(precond * image)), ('gx',...  402 us
    ppermute x33, starting transfers between devices, padded_2(): lax.ppermute(tail, axis, [(i, (i + 1) % count) for i in range(ends)])  93.8 us
    ppermute x33, waiting for transfers between devices, padded_2(): lax.ppermute(head, axis, [((i + 1) % count, i) for i in range(ends)])  90.9 us
    reduce_sum x10, other arithmetic, paired_dots(): jnp.sum(precond * image)  77.3 us
    ppermute x33, starting transfers between devices, padded_2(): lax.ppermute(head, axis, [((i + 1) % count, i) for i in range(ends)])  44 us
    slice x42, local copies, waits for them, and re-layouts, padded_2(): lax.slice_in_dim(cells, cells.shape[dim] - width, cells.shape[dim], axis=...  36.8 us
    div x10, other arithmetic, local(): precond = residual / total  33.2 us
  transfers between devices with their start and end apart: 66, of which 42 were waited for; matrix products, arithmetic and copies ran while one was open for 4% of the time, Pallas kernels for 0%

commit v1 on v0

v1 whole, which is shorter than its diff:
```python
import functools

import jax
import jax.numpy as jnp
from jax import lax
from jax.experimental import pallas as pl
from jax.experimental.pallas import tpu as pltpu
from jax.sharding import PartitionSpec as P

ITERS = 10
SIGMA = 0.75
AXES = ("gx", "gy", "gz")
MESH = pl.DeviceIdType.MESH
PAD = 8
TILE = 8
LANES = 128
HALF = LANES // 2
MOMENT_ROWS = 24


def krylov_coefficients(moments):
    zero = jnp.zeros_like(moments[0])
    one = zero + 1.0

    def shifted(values):
        out = [SIGMA * values[1]]
        for j in range(1, len(values) - 1):
            out.append(0.5 * SIGMA * (values[j + 1] + values[j - 1]))
        return out

    def times_j(coeffs):
        out = [zero] * (len(coeffs) + 1)
        for j, value in enumerate(coeffs):
            if j == 0:
                out[1] = out[1] + SIGMA * value
            else:
                out[j + 1] = out[j + 1] + 0.5 * SIGMA * value
                out[j - 1] = out[j - 1] + 0.5 * SIGMA * value
        return out

    z_dots, p_dots = list(moments), list(moments)
    z_poly, p_poly, x_poly = [one], [one], []
    rho = moments[0]
    for k in range(ITERS):
        moved = shifted(p_dots)
        image_dots = [p_dots[j] - moved[j] for j in range(len(moved))]
        moved = times_j(p_poly)
        image_poly = [(p_poly[j] if j <= k else zero) - moved[j] for j in range(k + 2)]
        product = p_poly[k] * image_dots[k]
        good = jnp.logical_and(rho > 0.0, product > 0.0)
        step = jnp.where(good, rho / jnp.where(good, product, 1.0), 0.0)
        x_poly = [(x_poly[j] if j < k else zero) + step * p_poly[j] for j in range(k + 1)]
        z_poly = [(z_poly[j] if j <= k else zero) - step * image_poly[j] for j in range(k + 2)]
        z_dots = [z_dots[j] - step * image_dots[j] for j in range(len(image_dots))]
        rho_next = jnp.maximum(z_poly[k + 1] * z_dots[k + 1], 0.0)
        mixing = jnp.where(good, rho_next / jnp.where(good, rho, 1.0), 0.0)
        p_poly = [z_poly[j] + (mixing * p_poly[j] if j <= k else zero) for j in range(k + 2)]
        p_dots = [z_dots[j] + mixing * p_dots[j] for j in range(len(image_dots))]
        rho = rho_next
    return x_poly, z_poly


def kernel(sizes, b_ref, c_ref, a_ref, x_ref, r_ref,
           field, weight, diag, ysend, yrecv, yhalo, zsend, zrecv, dots,
           parts_x, parts_y, parts_z, send_sem, recv_sem, sum_send, sum_recv):
    nx, nz, ny = x_ref.shape
    tiles = nz // TILE
    per_group = HALF // tiles
    groups = nx // per_group
    me = {axis: lax.axis_index(axis) for axis in AXES}
    inner = pl.ds(PAD, nz)

    barrier = pltpu.get_barrier_semaphore()
    greeted = 0
    for axis in AXES:
        for hop in range(1, sizes[axis]):
            peer = lax.rem(me[axis] + hop, sizes[axis])
            pl.semaphore_signal(barrier, inc=1, device_id={axis: peer}, device_id_type=MESH)
            greeted += 1
    pl.semaphore_wait(barrier, greeted)

    lane = lax.broadcasted_iota(jnp.int32, (TILE, LANES), 1)
    owner = ((lane + 1) // 2) % HALF
    even = lane % 2 == 0
    lane_wide = lax.broadcasted_iota(jnp.int32, (nz, LANES), 1)
    first, last = lane_wide == 0, lane_wide == LANES - 1

    def each_copy(slot, act):
        plan = {
            "gx": ((field.at[slot, 1, inner], field.at[slot, nx + 1, inner]),
                   (field.at[slot, nx, inner], field.at[slot, 0, inner])),
            "gy": ((ysend.at[slot], yrecv.at[slot, 1]), (ysend.at[slot], yrecv.at[slot, 0])),
            "gz": ((zsend.at[slot, 0], zrecv.at[slot, 1]), (zsend.at[slot, 1], zrecv.at[slot, 0])),
        }
        for number, axis in enumerate(AXES):
            for side in range(2):
                source, target = plan[axis][side]
                act(axis, side, source, target, slot, 2 * number + side)

    def descriptor(axis, side, source, target, slot, index):
        peer = me[axis] + (2 * side - 1)
        return pltpu.make_async_remote_copy(
            src_ref=source, dst_ref=target,
            send_sem=send_sem.at[slot, index], recv_sem=recv_sem.at[slot, index],
            device_id={axis: peer}, device_id_type=MESH)

    def has_peer(axis, side):
        return me[axis] > 0 if side == 0 else me[axis] < sizes[axis] - 1

    def start(axis, side, *rest):
        @pl.when(has_peer(axis, side))
        def _():
            descriptor(axis, side, *rest).start()

    def finish(axis, side, *rest):
        @pl.when(has_peer(axis, side))
        def _():
            descriptor(axis, side, *rest).wait_send()

        @pl.when(has_peer(axis, 1 - side))
        def _():
            descriptor(axis, side, *rest).wait_recv()

    def clear(slot, carry):
        plane = jnp.zeros((nz, ny), jnp.float32)
        for edge, at in ((me["gx"] == 0, 0), (me["gx"] == sizes["gx"] - 1, nx + 1)):
            @pl.when(edge)
            def _():
                field[slot, at, inner] = plane
        for edge, at in ((me["gy"] == 0, 0), (me["gy"] == sizes["gy"] - 1, 1)):
            @pl.when(edge)
            def _():
                yrecv[slot, at] = jnp.zeros(yrecv.shape[2:], jnp.float32)
        for edge, at in ((me["gz"] == 0, 0), (me["gz"] == sizes["gz"] - 1, 1)):
            @pl.when(edge)
            def _():
                zrecv[slot, at] = jnp.zeros(zrecv.shape[2:], jnp.float32)
        return carry

    lax.fori_loop(0, ITERS + 1, clear, 0)

    def put(slot, x, within, plane, packed):
        field[slot, x + 1, inner] = plane
        zsend[slot, 0, pl.ds(x, 1)] = plane[:1]
        zsend[slot, 1, pl.ds(x, 1)] = plane[nz - 1:]
        for tile in range(tiles):
            number = within * tiles + tile
            part = plane[tile * TILE:(tile + 1) * TILE]
            if number:
                part = pltpu.roll(part, 2 * number, 1)
            packed = jnp.where(owner == number, part, packed)
        return packed

    def exchange(slot):
        each_copy(slot, start)
        each_copy(slot, finish)
        for group in range(groups):
            yhalo[group] = jnp.where(even, pltpu.roll(yrecv[slot, 0, group], 1, 1),
                                     pltpu.roll(yrecv[slot, 1, group], LANES - 1, 1))
        for x in range(nx):
            field[slot, x + 1, PAD - 1:PAD] = zrecv[slot, 0, x:x + 1]
            field[slot, x + 1, PAD + nz:PAD + nz + 1] = zrecv[slot, 1, x:x + 1]

    def around(slot, x, group, within):
        here = field[slot, x + 1, inner]
        beside = yhalo[group]
        edge = []
        for tile in range(tiles):
            number = within * tiles + tile
            edge.append(pltpu.roll(beside, LANES - 2 * number, 1) if number else beside)
        edge = jnp.concatenate(edge, axis=0)
        return here, (
            field[slot, x + 2, inner],
            field[slot, x, inner],
            jnp.where(last, edge, pltpu.roll(here, LANES - 1, 1)),
            jnp.where(first, edge, pltpu.roll(here, 1, 1)),
            field[slot, x + 1, PAD + 1:PAD + 1 + nz],
            field[slot, x + 1, PAD - 1:PAD - 1 + nz],
        )

    def fold(plane):
        total = plane[:TILE]
        for tile in range(1, tiles):
            total = total + plane[tile * TILE:(tile + 1) * TILE]
        return total

    nothing = jnp.zeros((TILE, LANES), jnp.float32)

    def load(group, carry):
        packed = nothing
        for within in range(per_group):
            x = group * per_group + within
            packed = put(0, x, within, c_ref[x], packed)
        ysend[0, group] = packed
        return carry

    lax.fori_loop(0, groups, load, 0)
    exchange(0)

    def prepare(group, total):
        packed = nothing
        for within in range(per_group):
            x = group * per_group + within
            here, neighbours = around(0, x, group, within)
            faces = [0.5 * (here + other) for other in neighbours]
            diagonal = a_ref[x]
            for face in faces:
                diagonal = diagonal + face
            inverse = 1.0 / diagonal
            scale = (2.0 / SIGMA) * inverse
            for number, face in enumerate(faces):
                weight[number, x] = face * scale
            diag[x] = diagonal
            source = b_ref[x]
            precond = source / diagonal
            packed = put(1, x, within, precond, packed)
            total = total + fold(source * precond)
        ysend[1, group] = packed
        return total

    dots[0, 0] = lax.fori_loop(0, groups, prepare, nothing)

    def step(k, carry):
        slot = k + 1
        exchange(slot)
        scale = jnp.where(k == 0, 0.5, 1.0).astype(jnp.float32)
        keep = jnp.where(k == 0, 0.0, 1.0).astype(jnp.float32)

        def apply(group, totals):
            even_total, odd_total = totals
            packed = nothing
            for within in range(per_group):
                x = group * per_group + within
                here, neighbours = around(slot, x, group, within)
                image = weight[0, x] * neighbours[0]
                for number in range(1, 6):
                    image = image + weight[number, x] * neighbours[number]
                new = scale * image - keep * field[slot - 1, x + 1, inner]
                packed = put(slot + 1, x, within, new, packed)
                weighed = diag[x] * new
                even_total = even_total + fold(weighed * new)
                odd_total = odd_total + fold(weighed * here)
            ysend[slot + 1, group] = packed
            return even_total, odd_total

        even_total, odd_total = lax.fori_loop(0, groups, apply, (nothing, nothing))
        dots[k + 1, 0] = even_total
        dots[k, 1] = odd_total
        return carry

    lax.fori_loop(0, ITERS, step, 0)

    rows = [jnp.sum(dots[k, 0], axis=0, keepdims=True) for k in range(ITERS + 1)]
    rows += [jnp.sum(dots[k, 1], axis=0, keepdims=True) for k in range(ITERS)]
    rows += [jnp.zeros((1, LANES), jnp.float32)] * (MOMENT_ROWS - len(rows))
    sums = jnp.concatenate(rows, axis=0)
    base = 0
    for axis, parts in zip(AXES, (parts_x, parts_y, parts_z)):
        count = sizes[axis]
        parts[me[axis]] = sums
        copies = []
        for hop in range(1, count):
            copies.append(pltpu.make_async_remote_copy(
                src_ref=parts.at[me[axis]], dst_ref=parts.at[me[axis]],
                send_sem=sum_send.at[base], recv_sem=sum_recv.at[base],
                device_id={axis: lax.rem(me[axis] + hop, count)}, device_id_type=MESH))
            base += 1
        for copy in copies:
            copy.start()
        for hop, copy in enumerate(copies):
            came = lax.rem(me[axis] + (count - 1 - hop), count)
            copy.wait_send()
            pltpu.make_async_remote_copy(
                src_ref=parts.at[came], dst_ref=parts.at[came],
                send_sem=sum_send.at[base - count + 1 + hop],
                recv_sem=sum_recv.at[base - count + 1 + hop],
                device_id={axis: came}, device_id_type=MESH).wait_recv()
        sums = parts[0]
        for number in range(1, count):
            sums = sums + parts[number]

    sums = jnp.broadcast_to(jnp.sum(sums, axis=1, keepdims=True), (MOMENT_ROWS, LANES))
    evens = [sums[k:k + 1] for k in range(ITERS + 1)]
    odds = [sums[ITERS + 1 + k:ITERS + 2 + k] for k in range(ITERS)]
    moments = [evens[0], odds[0]]
    for k in range(1, ITERS + 1):
        moments.append(2.0 * evens[k] - moments[0])
        if k < ITERS:
            moments.append(2.0 * odds[k] - moments[1])
    x_poly, z_poly = krylov_coefficients(moments)

    def combine(x, carry):
        value = field[1, x + 1, inner]
        solution_field = x_poly[0] * value
        remainder = z_poly[0] * value
        for k in range(1, ITERS + 1):
            value = field[k + 1, x + 1, inner]
            if k < ITERS:
                solution_field = solution_field + x_poly[k] * value
            remainder = remainder + z_poly[k] * value
        x_ref[x] = solution_field
        r_ref[x] = remainder * diag[x]
        return carry

    lax.fori_loop(0, nx, combine, 0)


def local(sizes, right_side, conductivity, absorption):
    turned = [jnp.swapaxes(value, 1, 2) for value in (right_side, conductivity, absorption)]
    nx, nz, ny = turned[0].shape
    groups = nx * (nz // TILE) // HALF
    slots = ITERS + 2
    f32 = jnp.float32
    links = sum(sizes[axis] - 1 for axis in AXES)
    out = jax.ShapeDtypeStruct((nx, nz, ny), f32)
    vmem = pl.BlockSpec(memory_space=pltpu.VMEM)
    outs = pl.pallas_call(
        functools.partial(kernel, sizes),
        out_shape=(out, out),
        in_specs=[vmem] * 3,
        out_specs=(vmem, vmem),
        scratch_shapes=[
            pltpu.VMEM((slots, nx + 2, nz + 2 * PAD, ny), f32),
            pltpu.VMEM((6, nx, nz, ny), f32),
            pltpu.VMEM((nx, nz, ny), f32),
            pltpu.VMEM((slots, groups, TILE, LANES), f32),
            pltpu.VMEM((slots, 2, groups, TILE, LANES), f32),
            pltpu.VMEM((groups, TILE, LANES), f32),
            pltpu.VMEM((slots, 2, nx, ny), f32),
            pltpu.VMEM((slots, 2, nx, ny), f32),
            pltpu.VMEM((ITERS + 1, 2, TILE, LANES), f32),
            pltpu.VMEM((sizes["gx"], MOMENT_ROWS, LANES), f32),
            pltpu.VMEM((sizes["gy"], MOMENT_ROWS, LANES), f32),
            pltpu.VMEM((sizes["gz"], MOMENT_ROWS, LANES), f32),
            pltpu.SemaphoreType.DMA((slots, 6)),
            pltpu.SemaphoreType.DMA((slots, 6)),
            pltpu.SemaphoreType.DMA((links,)),
            pltpu.SemaphoreType.DMA((links,)),
        ],
        compiler_params=pltpu.CompilerParams(
            collective_id=0, has_side_effects=True, vmem_limit_bytes=60 * 1024 * 1024),
    )(*turned)
    return tuple(jnp.swapaxes(value, 1, 2) for value in outs)


def solution(mesh):
    sizes = dict(mesh.shape)
    return jax.shard_map(
        functools.partial(local, sizes),
        mesh=mesh,
        in_specs=(P(*AXES), P(*AXES), P(*AXES)),
        out_specs=(P(*AXES), P(*AXES)),
        check_vma=False,
    )
```

time: 917 us -> 89.7 us (0.10); the launches traced: 905 us -> 89.6 us
  blocking collectives: 402 us -> 0 us
  other arithmetic: 140 us -> 0 us
  starting transfers between devices: 138 us -> 0 us
  waiting for transfers between devices: 95.5 us -> 0 us
  local copies, waits for them, and re-layouts: 91.1 us -> 3.37 us
  Pallas kernels: 0 us -> 85.5 us
  between operations: 38 us -> 0.65 us
    psum x10 -> x0, blocking collectives: 402 us -> none  [paired_dots(): lax.psum((jnp.sum(residual * precond), jnp.sum(precond * image)), ('gx',...]
    ppermute x66 -> x0, starting transfers between devices: 138 us -> none  [the longest x33 93.8 us: padded_2(): lax.ppermute(tail, axis, [(i, (i + 1) % count) for i in range(ends)])]
    ppermute x66 -> x0, waiting for transfers between devices: 95.5 us -> none  [the longest x33 90.9 us: padded_2(): lax.ppermute(head, axis, [((i + 1) % count, i) for i in range(ends)])]
    pallas_call x0 -> x1, Pallas kernels: none -> 85.5 us  [local(): pl.pallas_call(functools.partial(kernel, sizes), out_shape=(out, out), in...]
    reduce_sum x10 -> x0, other arithmetic: 77.3 us -> none  [paired_dots(): jnp.sum(precond * image)]
    slice x64 -> x0, local copies, waits for them, and re-layouts: 54.6 us -> none  [the longest x42 36.8 us: padded_2(): lax.slice_in_dim(cells, cells.shape[dim] - width, cells.shape[dim], axis=...]
    div x10 -> x0, other arithmetic: 33.2 us -> none  [local(): precond = residual / total]
    ppermute x44 -> x0, local copies, waits for them, and re-layouts: 31.5 us -> none  [the longest x22 16.3 us: padded_2(): lax.ppermute(head, axis, [((i + 1) % count, i) for i in range(ends)])]
  transfers between devices with their start and end apart: 66 -> 0, of which waited for: 42 -> 0; matrix products, arithmetic and copies ran while one was open for 4% -> 0% of each run, Pallas kernels for 0% -> 0%
where the time goes in v1:
time: 89.7 us; the launch traced here: 89.6 us
  Pallas kernels  85.5 us (95%)
  local copies, waits for them, and re-layouts  3.37 us (4%)
    pallas_call x1, Pallas kernels, local(): pl.pallas_call(functools.partial(kernel, sizes), out_shape=(out, out), in...  85.5 us
    unnamed x4, local copies, waits for them, and re-layouts  3.37 us

profile of v1, /device:TPU:0, one launch (start us, length us, event | category | flops | bytes accessed | tf_op | source)
XLA Modules:
  0.0 89.6 jit_solution(12974668232550878696)
XLA Ops:
  0.6 85.5 %shard_map.50 = (f32[32,64,128]{2,1,0:T(8,128)}, f32[32,64,128]{2,1,0:T(8,128)}) custom-call(f32[32,64,128]{2,1,0:T(8,128)} %bitcast.5, f32[32,64,128]{2,1,0:T(8,128)} %bitcast.6, f32[32,64,128]{2,1,0:T(8,128)} %bitcast.7), custom_call_target="tpu_custom_call" | custom-call | tf_op jit(solution)/shard_map/pallas_call | solution.py:317
  86.2 0.0 copy-start
  86.2 2.4 %copy.7 = f32[32,128,64]{1,2,0:T(8,128)} copy(f32[32,128,64]{1,2,0:T(8,128)} %bitcast.9) | data formatting | bytes 2097152
  88.6 0.0 copy-done
  88.6 1.0 %copy.8 = f32[32,128,64]{1,2,0:T(8,128)} copy(f32[32,128,64]{1,2,0:T(8,128)S(1)} %bitcast.8) | data formatting | bytes 2097152
Async XLA Ops:
  86.2 2.4 %copy-start = (f32[32,64,128]{2,1,0:T(8,128)S(1)}, f32[32,64,128]{2,1,0:T(8,128)}, u32[]{:S(2)}) copy-start(f32[32,64,128]{2,1,0:T(8,128)} %get-tuple-element.5) | copy-start | bytes 3145732

commit v2 on v1

v2 whole, which is shorter than its diff:
```python
import functools

import jax
import jax.numpy as jnp
from jax import lax
from jax.experimental import pallas as pl
from jax.experimental.pallas import tpu as pltpu
from jax.sharding import PartitionSpec as P

ITERS = 10
AXES = ("gx", "gy", "gz")
MESH = pl.DeviceIdType.MESH
PAD = 8
TILE = 8
LANES = 128
HALF = LANES // 2
DOT_ROWS = 8


def kernel(sizes, b_ref, c_ref, a_ref, x_ref, r_ref,
           field, weight, diag, inverse, image_ref, direction_ref, along_ref,
           ysend, yrecv, yhalo, zsend, zrecv,
           parts_x, parts_y, parts_z, send_sem, recv_sem, sum_send, sum_recv):
    nx, nz, ny = x_ref.shape
    tiles = nz // TILE
    per_group = HALF // tiles
    groups = nx // per_group
    me = {axis: lax.axis_index(axis) for axis in AXES}
    inner = pl.ds(PAD, nz)

    barrier = pltpu.get_barrier_semaphore()
    greeted = 0
    for axis in AXES:
        for hop in range(1, sizes[axis]):
            peer = lax.rem(me[axis] + hop, sizes[axis])
            pl.semaphore_signal(barrier, inc=1, device_id={axis: peer}, device_id_type=MESH)
            greeted += 1
    pl.semaphore_wait(barrier, greeted)

    lane = lax.broadcasted_iota(jnp.int32, (TILE, LANES), 1)
    owner = ((lane + 1) // 2) % HALF
    even = lane % 2 == 0
    lane_wide = lax.broadcasted_iota(jnp.int32, (nz, LANES), 1)
    first, last = lane_wide == 0, lane_wide == LANES - 1

    def each_copy(slot, act):
        plan = {
            "gx": ((field.at[slot, 1, inner], field.at[slot, nx + 1, inner]),
                   (field.at[slot, nx, inner], field.at[slot, 0, inner])),
            "gy": ((ysend.at[slot], yrecv.at[slot, 1]), (ysend.at[slot], yrecv.at[slot, 0])),
            "gz": ((zsend.at[slot, 0], zrecv.at[slot, 1]), (zsend.at[slot, 1], zrecv.at[slot, 0])),
        }
        for number, axis in enumerate(AXES):
            for side in range(2):
                source, target = plan[axis][side]
                act(axis, side, source, target, slot, 2 * number + side)

    def descriptor(axis, side, source, target, slot, index):
        peer = me[axis] + (2 * side - 1)
        return pltpu.make_async_remote_copy(
            src_ref=source, dst_ref=target,
            send_sem=send_sem.at[slot, index], recv_sem=recv_sem.at[slot, index],
            device_id={axis: peer}, device_id_type=MESH)

    def has_peer(axis, side):
        return me[axis] > 0 if side == 0 else me[axis] < sizes[axis] - 1

    def start(axis, side, *rest):
        @pl.when(has_peer(axis, side))
        def _():
            descriptor(axis, side, *rest).start()

    def finish(axis, side, *rest):
        @pl.when(has_peer(axis, side))
        def _():
            descriptor(axis, side, *rest).wait_send()

        @pl.when(has_peer(axis, 1 - side))
        def _():
            descriptor(axis, side, *rest).wait_recv()

    def clear(slot, carry):
        plane = jnp.zeros((nz, ny), jnp.float32)
        for edge, at in ((me["gx"] == 0, 0), (me["gx"] == sizes["gx"] - 1, nx + 1)):
            @pl.when(edge)
            def _():
                field[slot, at, inner] = plane
        for edge, at in ((me["gy"] == 0, 0), (me["gy"] == sizes["gy"] - 1, 1)):
            @pl.when(edge)
            def _():
                yrecv[slot, at] = jnp.zeros(yrecv.shape[2:], jnp.float32)
        for edge, at in ((me["gz"] == 0, 0), (me["gz"] == sizes["gz"] - 1, 1)):
            @pl.when(edge)
            def _():
                zrecv[slot, at] = jnp.zeros(zrecv.shape[2:], jnp.float32)
        return carry

    lax.fori_loop(0, ITERS + 1, clear, 0)

    def put(slot, x, within, plane, packed):
        field[slot, x + 1, inner] = plane
        zsend[slot, 0, pl.ds(x, 1)] = plane[:1]
        zsend[slot, 1, pl.ds(x, 1)] = plane[nz - 1:]
        for tile in range(tiles):
            number = within * tiles + tile
            part = plane[tile * TILE:(tile + 1) * TILE]
            if number:
                part = pltpu.roll(part, 2 * number, 1)
            packed = jnp.where(owner == number, part, packed)
        return packed

    def exchange(slot):
        each_copy(slot, start)
        each_copy(slot, finish)
        for group in range(groups):
            yhalo[group] = jnp.where(even, pltpu.roll(yrecv[slot, 0, group], 1, 1),
                                     pltpu.roll(yrecv[slot, 1, group], LANES - 1, 1))
        for x in range(nx):
            field[slot, x + 1, PAD - 1:PAD] = zrecv[slot, 0, x:x + 1]
            field[slot, x + 1, PAD + nz:PAD + nz + 1] = zrecv[slot, 1, x:x + 1]

    def around(slot, x, group, within):
        here = field[slot, x + 1, inner]
        beside = yhalo[group]
        edge = []
        for tile in range(tiles):
            number = within * tiles + tile
            edge.append(pltpu.roll(beside, LANES - 2 * number, 1) if number else beside)
        edge = jnp.concatenate(edge, axis=0)
        return here, (
            field[slot, x + 2, inner],
            field[slot, x, inner],
            jnp.where(last, edge, pltpu.roll(here, LANES - 1, 1)),
            jnp.where(first, edge, pltpu.roll(here, 1, 1)),
            field[slot, x + 1, PAD + 1:PAD + 1 + nz],
            field[slot, x + 1, PAD - 1:PAD - 1 + nz],
        )

    def fold(plane):
        total = plane[:TILE]
        for tile in range(1, tiles):
            total = total + plane[tile * TILE:(tile + 1) * TILE]
        return total

    nothing = jnp.zeros((TILE, LANES), jnp.float32)

    def load(group, carry):
        packed = nothing
        for within in range(per_group):
            x = group * per_group + within
            packed = put(0, x, within, c_ref[x], packed)
        ysend[0, group] = packed
        return carry

    lax.fori_loop(0, groups, load, 0)
    exchange(0)

    def prepare(group, carry):
        packed = nothing
        for within in range(per_group):
            x = group * per_group + within
            here, neighbours = around(0, x, group, within)
            faces = [0.5 * (here + other) for other in neighbours]
            diagonal = a_ref[x]
            for number, face in enumerate(faces):
                diagonal = diagonal + face
                weight[number, x] = face
            diag[x] = diagonal
            reciprocal = 1.0 / diagonal
            inverse[x] = reciprocal
            source = b_ref[x]
            r_ref[x] = source
            blank = jnp.zeros_like(source)
            x_ref[x] = blank
            direction_ref[x] = blank
            along_ref[x] = blank
            packed = put(1, x, within, source * reciprocal, packed)
        ysend[1, group] = packed
        return carry

    lax.fori_loop(0, groups, prepare, 0)

    def all_sums(k, sums):
        base = 0
        for axis, parts in zip(AXES, (parts_x, parts_y, parts_z)):
            count = sizes[axis]
            parts[k, me[axis]] = sums
            sends, arrivals = [], []
            for hop in range(1, count):
                for whose, device, out in (
                    (me[axis], lax.rem(me[axis] + hop, count), sends),
                    (lax.rem(me[axis] + count - hop, count),) * 2 + (arrivals,),
                ):
                    out.append(pltpu.make_async_remote_copy(
                        src_ref=parts.at[k, whose], dst_ref=parts.at[k, whose],
                        send_sem=sum_send.at[k, base], recv_sem=sum_recv.at[k, base],
                        device_id={axis: device}, device_id_type=MESH))
                base += 1
            for copy in sends:
                copy.start()
            for copy, arrival in zip(sends, arrivals):
                copy.wait_send()
                arrival.wait_recv()
            sums = parts[k, 0]
            for number in range(1, count):
                sums = sums + parts[k, number]
        return jnp.broadcast_to(jnp.sum(sums, axis=1, keepdims=True), (DOT_ROWS, LANES))

    def iteration(k, carry):
        rho_now, step_size = carry
        slot = k + 1
        exchange(slot)

        def apply(group, totals):
            rho_total, product_total = totals
            for within in range(per_group):
                x = group * per_group + within
                here, neighbours = around(slot, x, group, within)
                beside = weight[0, x] * neighbours[0]
                for number in range(1, 6):
                    beside = beside + weight[number, x] * neighbours[number]
                image = diag[x] * here - beside
                image_ref[x] = image
                rho_total = rho_total + fold(r_ref[x] * here)
                product_total = product_total + fold(image * here)
            return rho_total, product_total

        rho_total, product_total = lax.fori_loop(0, groups, apply, (nothing, nothing))
        sums = all_sums(k, jnp.concatenate([
            jnp.sum(rho_total, axis=0, keepdims=True),
            jnp.sum(product_total, axis=0, keepdims=True),
            jnp.zeros((DOT_ROWS - 2, LANES), jnp.float32)], axis=0))
        rho_next, product = sums[:1], sums[1:2]
        mixing = jnp.where(k == 0, 0.0, rho_next / rho_now)
        step_next = rho_next / (product - mixing * rho_next / step_size)

        def update(group, carry):
            packed = nothing
            for within in range(per_group):
                x = group * per_group + within
                direction = field[slot, x + 1, inner] + mixing * direction_ref[x]
                along = image_ref[x] + mixing * along_ref[x]
                direction_ref[x] = direction
                along_ref[x] = along
                x_ref[x] = x_ref[x] + step_next * direction
                residual = r_ref[x] - step_next * along
                r_ref[x] = residual
                packed = put(slot + 1, x, within, residual * inverse[x], packed)
            ysend[slot + 1, group] = packed
            return carry

        lax.fori_loop(0, groups, update, 0)
        return rho_next, step_next

    one = jnp.ones((1, LANES), jnp.float32)
    lax.fori_loop(0, ITERS, iteration, (one, one))


def local(sizes, right_side, conductivity, absorption):
    turned = [jnp.swapaxes(value, 1, 2) for value in (right_side, conductivity, absorption)]
    nx, nz, ny = turned[0].shape
    groups = nx * (nz // TILE) // HALF
    slots = ITERS + 2
    f32 = jnp.float32
    links = sum(sizes[axis] - 1 for axis in AXES)
    out = jax.ShapeDtypeStruct((nx, nz, ny), f32)
    vmem = pl.BlockSpec(memory_space=pltpu.VMEM)
    outs = pl.pallas_call(
        functools.partial(kernel, sizes),
        out_shape=(out, out),
        in_specs=[vmem] * 3,
        out_specs=(vmem, vmem),
        scratch_shapes=[
            pltpu.VMEM((slots, nx + 2, nz + 2 * PAD, ny), f32),
            pltpu.VMEM((6, nx, nz, ny), f32),
            *[pltpu.VMEM((nx, nz, ny), f32) for _ in range(5)],
            pltpu.VMEM((slots, groups, TILE, LANES), f32),
            pltpu.VMEM((slots, 2, groups, TILE, LANES), f32),
            pltpu.VMEM((groups, TILE, LANES), f32),
            pltpu.VMEM((slots, 2, nx, ny), f32),
            pltpu.VMEM((slots, 2, nx, ny), f32),
            pltpu.VMEM((ITERS, sizes["gx"], DOT_ROWS, LANES), f32),
            pltpu.VMEM((ITERS, sizes["gy"], DOT_ROWS, LANES), f32),
            pltpu.VMEM((ITERS, sizes["gz"], DOT_ROWS, LANES), f32),
            pltpu.SemaphoreType.DMA((slots, 6)),
            pltpu.SemaphoreType.DMA((slots, 6)),
            pltpu.SemaphoreType.DMA((ITERS, links)),
            pltpu.SemaphoreType.DMA((ITERS, links)),
        ],
        compiler_params=pltpu.CompilerParams(
            collective_id=0, has_side_effects=True, vmem_limit_bytes=60 * 1024 * 1024),
    )(*turned)
    return tuple(jnp.swapaxes(value, 1, 2) for value in outs)


def solution(mesh):
    sizes = dict(mesh.shape)
    return jax.shard_map(
        functools.partial(local, sizes),
        mesh=mesh,
        in_specs=(P(*AXES), P(*AXES), P(*AXES)),
        out_specs=(P(*AXES), P(*AXES)),
        check_vma=False,
    )
```

time: 89.7 us -> 152 us (1.69)
  Pallas kernels: 85.5 us -> 148 us
    pallas_call x1, Pallas kernels: 85.5 us -> 148 us  [local(): pl.pallas_call(functools.partial(kernel, sizes), out_shape=(out, out), in...]
where the time goes in v2:
time: 152 us
  Pallas kernels  148 us (97%)
  local copies, waits for them, and re-layouts  3.37 us (2%)
    pallas_call x1, Pallas kernels, local(): pl.pallas_call(functools.partial(kernel, sizes), out_shape=(out, out), in...  148 us
    unnamed x4, local copies, waits for them, and re-layouts  3.37 us

profile of v2, /device:TPU:0, one launch (start us, length us, event | category | flops | bytes accessed | tf_op | source)
XLA Modules:
  0.0 151.6 jit_solution(14159834437258137987)
XLA Ops:
  0.6 147.6 %shard_map.50 = (f32[32,64,128]{2,1,0:T(8,128)}, f32[32,64,128]{2,1,0:T(8,128)}) custom-call(f32[32,64,128]{2,1,0:T(8,128)} %bitcast.5, f32[32,64,128]{2,1,0:T(8,128)} %bitcast.6, f32[32,64,128]{2,1,0:T(8,128)} %bitcast.7), custom_call_target="tpu_custom_call" | custom-call | tf_op jit(solution)/shard_map/pallas_call | solution.py:268
  148.2 0.0 copy-start
  148.2 2.4 %copy.7 = f32[32,128,64]{1,2,0:T(8,128)} copy(f32[32,128,64]{1,2,0:T(8,128)} %bitcast.9) | data formatting | bytes 2097152
  150.6 0.0 copy-done
  150.6 1.0 copy.8
Async XLA Ops:
  148.2 2.4 %copy-start = (f32[32,64,128]{2,1,0:T(8,128)S(1)}, f32[32,64,128]{2,1,0:T(8,128)}, u32[]{:S(2)}) copy-start(f32[32,64,128]{2,1,0:T(8,128)} %get-tuple-element.5) | copy-start | bytes 3145732

commit v3 on v2

--- a/solution.py
+++ b/solution.py
@@ -1,4 +1,5 @@
 import functools
+import math
 
 import jax
 import jax.numpy as jnp
@@ -9,6 +10,7 @@
 
 ITERS = 10
 AXES = ("gx", "gy", "gz")
+STAGES = (("gx", "gy"), ("gz",))
 MESH = pl.DeviceIdType.MESH
 PAD = 8
 TILE = 8
@@ -20,7 +22,7 @@
 def kernel(sizes, b_ref, c_ref, a_ref, x_ref, r_ref,
            field, weight, diag, inverse, image_ref, direction_ref, along_ref,
            ysend, yrecv, yhalo, zsend, zrecv,
-           parts_x, parts_y, parts_z, send_sem, recv_sem, sum_send, sum_recv):
+           parts_first, parts_last, send_sem, recv_sem, sum_send, sum_recv):
     nx, nz, ny = x_ref.shape
     tiles = nz // TILE
     per_group = HALF // tiles
@@ -29,11 +31,26 @@
     inner = pl.ds(PAD, nz)
 
     barrier = pltpu.get_barrier_semaphore()
+    def mine(axes):
+        index, count = 0, 1
+        for axis in axes:
+            index = index * sizes[axis] + me[axis]
+            count = count * sizes[axis]
+        return index, count
+
+    def place(axes, index):
+        where = {}
+        for axis in reversed(axes):
+            where[axis] = lax.rem(index, sizes[axis])
+            index = lax.div(index, sizes[axis])
+        return where
+
     greeted = 0
-    for axis in AXES:
-        for hop in range(1, sizes[axis]):
-            peer = lax.rem(me[axis] + hop, sizes[axis])
-            pl.semaphore_signal(barrier, inc=1, device_id={axis: peer}, device_id_type=MESH)
+    for axes in STAGES:
+        index, count = mine(axes)
+        for hop in range(1, count):
+            peer = place(axes, lax.rem(index + hop, count))
+            pl.semaphore_signal(barrier, inc=1, device_id=peer, device_id_type=MESH)
             greeted += 1
     pl.semaphore_wait(barrier, greeted)
 
@@ -182,19 +199,18 @@
 
     def all_sums(k, sums):
         base = 0
-        for axis, parts in zip(AXES, (parts_x, parts_y, parts_z)):
-            count = sizes[axis]
-            parts[k, me[axis]] = sums
+        for axes, parts in zip(STAGES, (parts_first, parts_last)):
+            index, count = mine(axes)
+            parts[k, index] = sums
             sends, arrivals = [], []
             for hop in range(1, count):
-                for whose, device, out in (
-                    (me[axis], lax.rem(me[axis] + hop, count), sends),
-                    (lax.rem(me[axis] + count - hop, count),) * 2 + (arrivals,),
-                ):
+                behind = lax.rem(index + count - hop, count)
+                ahead = lax.rem(index + hop, count)
+                for whose, device, out in ((index, ahead, sends), (behind, behind, arrivals)):
                     out.append(pltpu.make_async_remote_copy(
                         src_ref=parts.at[k, whose], dst_ref=parts.at[k, whose],
                         send_sem=sum_send.at[k, base], recv_sem=sum_recv.at[k, base],
-                        device_id={axis: device}, device_id_type=MESH))
+                        device_id=place(axes, device), device_id_type=MESH))
                 base += 1
             for copy in sends:
                 copy.start()
@@ -262,7 +278,8 @@
     groups = nx * (nz // TILE) // HALF
     slots = ITERS + 2
     f32 = jnp.float32
-    links = sum(sizes[axis] - 1 for axis in AXES)
+    counts = [math.prod(sizes[axis] for axis in axes) for axes in STAGES]
+    links = sum(count - 1 for count in counts)
     out = jax.ShapeDtypeStruct((nx, nz, ny), f32)
     vmem = pl.BlockSpec(memory_space=pltpu.VMEM)
     outs = pl.pallas_call(
@@ -279,9 +296,7 @@
             pltpu.VMEM((groups, TILE, LANES), f32),
             pltpu.VMEM((slots, 2, nx, ny), f32),
             pltpu.VMEM((slots, 2, nx, ny), f32),
-            pltpu.VMEM((ITERS, sizes["gx"], DOT_ROWS, LANES), f32),
-            pltpu.VMEM((ITERS, sizes["gy"], DOT_ROWS, LANES), f32),
-            pltpu.VMEM((ITERS, sizes["gz"], DOT_ROWS, LANES), f32),
+            *[pltpu.VMEM((ITERS, count, DOT_ROWS, LANES), f32) for count in counts],
             pltpu.SemaphoreType.DMA((slots, 6)),
             pltpu.SemaphoreType.DMA((slots, 6)),
             pltpu.SemaphoreType.DMA((ITERS, links)),

time: 152 us -> 145 us (0.954)
  Pallas kernels: 148 us -> 141 us
    pallas_call x1, Pallas kernels: 148 us -> 141 us  [local(): pl.pallas_call(functools.partial(kernel, sizes), out_shape=(out, out), in...]
where the time goes in v3:
time: 145 us
  Pallas kernels  141 us (97%)
  local copies, waits for them, and re-layouts  3.37 us (2%)
    pallas_call x1, Pallas kernels, local(): pl.pallas_call(functools.partial(kernel, sizes), out_shape=(out, out), in...  141 us
    unnamed x4, local copies, waits for them, and re-layouts  3.37 us

profile of v3, /device:TPU:0, one launch (start us, length us, event | category | flops | bytes accessed | tf_op | source)
XLA Modules:
  0.0 144.8 jit_solution(8257021789280682737)
XLA Ops:
  0.6 140.8 %shard_map.50 = (f32[32,64,128]{2,1,0:T(8,128)}, f32[32,64,128]{2,1,0:T(8,128)}) custom-call(f32[32,64,128]{2,1,0:T(8,128)} %bitcast.5, f32[32,64,128]{2,1,0:T(8,128)} %bitcast.6, f32[32,64,128]{2,1,0:T(8,128)} %bitcast.7), custom_call_target="tpu_custom_call" | custom-call | tf_op jit(solution)/shard_map/pallas_call | solution.py:285
  141.4 0.0 copy-start
  141.4 2.4 %copy.7 = f32[32,128,64]{1,2,0:T(8,128)} copy(f32[32,128,64]{1,2,0:T(8,128)} %bitcast.9) | data formatting | bytes 2097152
  143.8 0.0 copy-done
  143.8 1.0 copy.8
Async XLA Ops:
  141.4 2.4 %copy-start = (f32[32,64,128]{2,1,0:T(8,128)S(1)}, f32[32,64,128]{2,1,0:T(8,128)}, u32[]{:S(2)}) copy-start(f32[32,64,128]{2,1,0:T(8,128)} %get-tuple-element.5) | copy-start | bytes 3145732

commit v4 on v3

--- a/solution.py
+++ b/solution.py
@@ -10,7 +10,7 @@
 
 ITERS = 10
 AXES = ("gx", "gy", "gz")
-STAGES = (("gx", "gy"), ("gz",))
+STAGES = (("gx", "gy", "gz"),)
 MESH = pl.DeviceIdType.MESH
 PAD = 8
 TILE = 8
@@ -22,7 +22,7 @@
 def kernel(sizes, b_ref, c_ref, a_ref, x_ref, r_ref,
            field, weight, diag, inverse, image_ref, direction_ref, along_ref,
            ysend, yrecv, yhalo, zsend, zrecv,
-           parts_first, parts_last, send_sem, recv_sem, sum_send, sum_recv):
+           parts_all, send_sem, recv_sem, sum_send, sum_recv):
     nx, nz, ny = x_ref.shape
     tiles = nz // TILE
     per_group = HALF // tiles
@@ -199,7 +199,7 @@
 
     def all_sums(k, sums):
         base = 0
-        for axes, parts in zip(STAGES, (parts_first, parts_last)):
+        for axes, parts in zip(STAGES, (parts_all,)):
             index, count = mine(axes)
             parts[k, index] = sums
             sends, arrivals = [], []

time: 145 us -> 136 us (0.938)
  Pallas kernels: 141 us -> 132 us
    pallas_call x1, Pallas kernels: 141 us -> 132 us  [local(): pl.pallas_call(functools.partial(kernel, sizes), out_shape=(out, out), in...]
where the time goes in v4:
time: 136 us
  Pallas kernels  132 us (97%)
  local copies, waits for them, and re-layouts  3.37 us (2%)
    pallas_call x1, Pallas kernels, local(): pl.pallas_call(functools.partial(kernel, sizes), out_shape=(out, out), in...  132 us
    unnamed x4, local copies, waits for them, and re-layouts  3.37 us

profile of v4, /device:TPU:0, one launch (start us, length us, event | category | flops | bytes accessed | tf_op | source)
XLA Modules:
  0.0 135.7 jit_solution(5778512685125600046)
XLA Ops:
  0.6 131.7 %shard_map.50 = (f32[32,64,128]{2,1,0:T(8,128)}, f32[32,64,128]{2,1,0:T(8,128)}) custom-call(f32[32,64,128]{2,1,0:T(8,128)} %bitcast.5, f32[32,64,128]{2,1,0:T(8,128)} %bitcast.6, f32[32,64,128]{2,1,0:T(8,128)} %bitcast.7), custom_call_target="tpu_custom_call" | custom-call | tf_op jit(solution)/shard_map/pallas_call | solution.py:285
  132.3 0.0 copy-start
  132.3 2.4 %copy.7 = f32[32,128,64]{1,2,0:T(8,128)} copy(f32[32,128,64]{1,2,0:T(8,128)} %bitcast.9) | data formatting | bytes 2097152
  134.7 0.0 copy-done
  134.7 1.0 copy.8
Async XLA Ops:
  132.3 2.4 %copy-start = (f32[32,64,128]{2,1,0:T(8,128)S(1)}, f32[32,64,128]{2,1,0:T(8,128)}, u32[]{:S(2)}) copy-start(f32[32,64,128]{2,1,0:T(8,128)} %get-tuple-element.5) | copy-start | bytes 3145732
